TPU v7x, 32 devices: a whole 2x2x4 slice. The times are simulated.
32 devices in a mesh: seq: 8 (over z, x), head: 4 (over y, core).
Axes of the slice: x: 2, y: 2, z: 4, core: 2. Of those that a mesh axis runs over, the one named last changes fastest.
Arguments:
- query_rows: bfloat16 [16384, 1024], P('seq', 'head'), may hold values from -8 to 8
- key_rows: bfloat16 [16384, 1024], P('seq', 'head'), may hold values from -6 to 6
- value_rows: bfloat16 [16384, 1024], P('seq', 'head'), may hold values from -12 to 12
- out_grad: bfloat16 [16384, 1024], P('seq', 'head'), may hold values from -12 to 12
- block_perm: int32 [8, 64], P('head'), may hold values from 0 to 63, as said below
- cut_count: int32 [8], P('head'), may hold values from 1 to 4, as said below
- norm_gain: float32 [1024], P('head'), may hold values from 0.1 to 1.9
Outputs:
- normed_out: bfloat16 [16384, 1024], P('seq', 'head')
- query_grad: bfloat16 [16384, 1024], P('seq', 'head')
- key_grad: bfloat16 [16384, 1024], P('seq', 'head')
- value_grad: bfloat16 [16384, 1024], P('seq', 'head')
- gain_grad: float32 [1024], P('head')
Inputs may be any that keep to these rules, and one draw needn't show every extreme that they name: `block_perm`: each row is a permutation of 0 to 63. For every head, of the 8 blocks d * 8 to (d + 1) * 8 - 1, at most 1 are paired with blocks of one range s * 8 to (s + 1) * 8 - 1, and some pair (d, s) reaches 1. `cut_count`: some head has exactly 4.
All inputs are finite; a program needn't handle non-finite values.
Results may differ from a plain program's by a relative error of at most 0.0071.
Values may be sent and summed in bfloat16 or wider, within the bound.
A program may use at most 128 MiB of HBM per device.

v0:
```python
from functools import partial
import jax
import jax.numpy as jnp
from jax import lax
from jax.sharding import PartitionSpec as P

BLOCK = 256
KCUT = 4


def split_heads(rows, heads):
    tokens = rows.shape[0]
    width = rows.shape[1] // heads
    return rows.reshape(tokens // BLOCK, BLOCK, heads, width).transpose(2, 0, 1, 3)


def merge_heads(parts):
    return parts.transpose(1, 2, 0, 3).reshape(
        parts.shape[1] * parts.shape[2], parts.shape[0] * parts.shape[3]
    )


def to_slots(rows, slot_of, count):
    match = slot_of[:, None, :] == jnp.arange(count)[None, :, None]
    chosen = jnp.sum(jnp.where(match, jnp.arange(rows.shape[1])[None, None, :], 0), axis=2)
    filled = jnp.any(match, axis=2)
    picked = jax.vmap(lambda piece, which: piece[which])(rows, chosen)
    shape = filled.shape + (1,) * (rows.ndim - 2)
    return jnp.where(filled.reshape(shape), picked, jnp.zeros_like(picked))


def from_slots(slot_rows, slot_of):
    return jax.vmap(lambda piece, which: piece[which])(slot_rows, slot_of)


def attend(query, own_rows, paired_rows, cutoff_rows, live, scale):
    width = query.shape[-1]
    span = own_rows.shape[1]
    count = cutoff_rows.shape[0]
    own = jnp.einsum(
        "gqd,gkd->gqk", query, own_rows[..., :width], preferred_element_type=jnp.float32
    )
    pair = jnp.einsum(
        "gqd,gkd->gqk", query, paired_rows[..., :width], preferred_element_type=jnp.float32
    )
    cut = jnp.einsum(
        "gqd,ckd->gqck", query, cutoff_rows[..., :width], preferred_element_type=jnp.float32
    )
    cut = cut.reshape(query.shape[0], query.shape[1], count * span)
    scores = jnp.concatenate([own, pair, cut], axis=-1) * scale
    open_keys = jnp.concatenate([jnp.ones((2 * span,), jnp.bool_), jnp.repeat(live, span)])
    scores = jnp.where(open_keys, scores, -1e30)
    top = jnp.max(scores, axis=-1)
    weights = jnp.exp(scores - top[..., None])
    total = jnp.sum(weights, axis=-1)
    return (weights / total[..., None], top, total)


def forward_head(query, own_rows, paired_rows, cutoff_rows, live, scale):
    width = query.shape[-1]
    span = query.shape[1]
    groups = query.shape[0] // 2
    count = cutoff_rows.shape[0]

    def forward_step(pieces):
        query_part, own_part, pair_part = pieces
        prob, top, total = attend(query_part, own_part, pair_part, cutoff_rows, live, scale)
        weights = prob.astype(jnp.bfloat16)
        result = jnp.einsum(
            "gqk,gkd->gqd",
            weights[..., :span],
            own_part[..., width:],
            preferred_element_type=jnp.float32,
        )
        result = result + jnp.einsum(
            "gqk,gkd->gqd",
            weights[..., span : 2 * span],
            pair_part[..., width:],
            preferred_element_type=jnp.float32,
        )
        cut_weight = weights[..., 2 * span :].reshape(2, span, count, span)
        result = result + jnp.einsum(
            "gqck,ckd->gqd",
            cut_weight,
            cutoff_rows[..., width:],
            preferred_element_type=jnp.float32,
        )
        return result.astype(jnp.bfloat16)

    result = lax.map(
        forward_step,
        (
            query.reshape(groups, 2, span, width),
            own_rows.reshape(groups, 2, span, 2 * width),
            paired_rows.reshape(groups, 2, span, 2 * width),
        ),
    )
    return result.reshape(query.shape)


def backward_head(query, own_rows, paired_rows, cutoff_rows, live, cotangent, scale):
    width = query.shape[-1]
    span = query.shape[1]
    groups = query.shape[0] // 2
    count = cutoff_rows.shape[0]

    def backward_step(carry, pieces):
        query_part, own_part, pair_part, cot_part = pieces
        prob, top, total = attend(query_part, own_part, pair_part, cutoff_rows, live, scale)
        weights = prob.astype(jnp.bfloat16)
        dprob = jnp.concatenate(
            [
                jnp.einsum(
                    "gqd,gkd->gqk",
                    cot_part,
                    own_part[..., width:],
                    preferred_element_type=jnp.float32,
                ),
                jnp.einsum(
                    "gqd,gkd->gqk",
                    cot_part,
                    pair_part[..., width:],
                    preferred_element_type=jnp.float32,
                ),
                jnp.einsum(
                    "gqd,ckd->gqck",
                    cot_part,
                    cutoff_rows[..., width:],
                    preferred_element_type=jnp.float32,
                ).reshape(2, span, count * span),
            ],
            axis=-1,
        )
        delta = jnp.sum(prob * dprob, axis=-1)
        dscore = (prob * (dprob - delta[..., None]) * scale).astype(jnp.bfloat16)
        cut_score = dscore[..., 2 * span :].reshape(2, span, count, span)
        cut_weight = weights[..., 2 * span :].reshape(2, span, count, span)
        query_grad = jnp.einsum(
            "gqk,gkd->gqd",
            dscore[..., :span],
            own_part[..., :width],
            preferred_element_type=jnp.float32,
        )
        query_grad = query_grad + jnp.einsum(
            "gqk,gkd->gqd",
            dscore[..., span : 2 * span],
            pair_part[..., :width],
            preferred_element_type=jnp.float32,
        )
        query_grad = query_grad + jnp.einsum(
            "gqck,ckd->gqd", cut_score, cutoff_rows[..., :width], preferred_element_type=jnp.float32
        )
        own_grad = jnp.concatenate(
            [
                jnp.einsum(
                    "gqk,gqd->gkd",
                    dscore[..., :span],
                    query_part,
                    preferred_element_type=jnp.float32,
                ),
                jnp.einsum(
                    "gqk,gqd->gkd",
                    weights[..., :span],
                    cot_part,
                    preferred_element_type=jnp.float32,
                ),
            ],
            axis=-1,
        )
        pair_grad = jnp.concatenate(
            [
                jnp.einsum(
                    "gqk,gqd->gkd",
                    dscore[..., span : 2 * span],
                    query_part,
                    preferred_element_type=jnp.float32,
                ),
                jnp.einsum(
                    "gqk,gqd->gkd",
                    weights[..., span : 2 * span],
                    cot_part,
                    preferred_element_type=jnp.float32,
                ),
            ],
            axis=-1,
        )
        cut_grad = jnp.concatenate(
            [
                jnp.einsum(
                    "gqck,gqd->ckd", cut_score, query_part, preferred_element_type=jnp.float32
                ),
                jnp.einsum(
                    "gqck,gqd->ckd", cut_weight, cot_part, preferred_element_type=jnp.float32
                ),
            ],
            axis=-1,
        )
        return (
            carry + cut_grad,
            (query_grad.astype(jnp.bfloat16), own_grad, pair_grad, top, total, delta),
        )

    start = jnp.zeros((count, span, 2 * width), jnp.float32)
    cut_sum, outputs = lax.scan(
        backward_step,
        start,
        (
            query.reshape(groups, 2, span, width),
            own_rows.reshape(groups, 2, span, 2 * width),
            paired_rows.reshape(groups, 2, span, 2 * width),
            cotangent.reshape(groups, 2, span, width),
        ),
    )
    query_grad, own_grad, pair_grad, top, total, delta = outputs
    blocks = query.shape[0]
    return (
        query_grad.reshape(query.shape),
        own_grad.reshape(own_rows.shape),
        pair_grad.reshape(own_rows.shape),
        cut_sum,
        top.reshape(blocks, span),
        total.reshape(blocks, span),
        delta.reshape(blocks, span),
    )


def owner_pair(query, cotangent, top, total, delta, own_rows, scale):
    width = query.shape[-1]
    scores = (
        jnp.einsum("jqd,jkd->jqk", query, own_rows[..., :width], preferred_element_type=jnp.float32)
        * scale
    )
    prob = jnp.exp(scores - top[..., None]) / total[..., None]
    dprob = jnp.einsum(
        "jqd,jkd->jqk", cotangent, own_rows[..., width:], preferred_element_type=jnp.float32
    )
    dscore = (prob * (dprob - delta[..., None]) * scale).astype(jnp.bfloat16)
    return jnp.concatenate(
        [
            jnp.einsum("jqk,jqd->jkd", dscore, query, preferred_element_type=jnp.float32),
            jnp.einsum(
                "jqk,jqd->jkd",
                prob.astype(jnp.bfloat16),
                cotangent,
                preferred_element_type=jnp.float32,
            ),
        ],
        axis=-1,
    )


def body(query_rows, key_rows, value_rows, out_grad, block_perm, cut_count, norm_gain):
    heads = block_perm.shape[0]
    width = query_rows.shape[1] // heads
    blocks = query_rows.shape[0] // BLOCK
    seq_count = lax.axis_size("seq")
    head_count = lax.axis_size("head")
    capacity = (blocks + seq_count - 1) // seq_count
    slot_count = seq_count * capacity
    scale = width ** (-0.5)
    position = lax.axis_index("seq")
    query_h = split_heads(query_rows, heads)
    grad_h = split_heads(out_grad, heads)
    own_rows = jnp.concatenate(
        [split_heads(key_rows, heads), split_heads(value_rows, heads)], axis=-1
    )
    local_perm = lax.dynamic_slice_in_dim(block_perm, position * blocks, blocks, 1)
    source_dev = local_perm // blocks
    lower = jnp.arange(blocks)[:, None] > jnp.arange(blocks)[None, :]
    same_source = source_dev[:, :, None] == source_dev[:, None, :]
    recv_slot = source_dev * capacity + jnp.sum(same_source & lower[None], axis=2)
    owned = position * blocks + jnp.arange(blocks)
    hits = block_perm[:, None, :] == owned[None, :, None]
    dest_global = jnp.sum(
        jnp.where(hits, jnp.arange(block_perm.shape[1])[None, None, :], 0), axis=2
    )
    dest_dev = dest_global // blocks
    dest_local = dest_global % blocks
    before = (dest_dev[:, :, None] == dest_dev[:, None, :]) & (
        dest_local[:, None, :] < dest_local[:, :, None]
    )
    send_slot = dest_dev * capacity + jnp.sum(before, axis=2)
    own_send = to_slots(own_rows, send_slot, slot_count)
    query_send = to_slots(query_h, recv_slot, slot_count)
    own_recv, query_recv = (
        lax.all_to_all(own_send, "seq", split_axis=1, concat_axis=1, tiled=True),
        lax.all_to_all(query_send, "seq", split_axis=1, concat_axis=1, tiled=True),
    )
    query_owner = from_slots(query_recv, send_slot)
    paired_rows = from_slots(own_recv, recv_slot)
    cut_global = block_perm[:, :KCUT]
    cut_dev = cut_global // blocks
    cut_local = cut_global % blocks
    cut_pick = jax.vmap(lambda piece, which: piece[which])(own_rows, cut_local)
    cut_pick = jnp.where(
        (cut_dev == position)[:, :, None, None], cut_pick, jnp.zeros_like(cut_pick)
    )
    cutoff_rows = lax.psum(cut_pick.astype(jnp.float32).astype(jnp.bfloat16), "seq")
    live = jnp.arange(KCUT)[None, :] < cut_count[:, None]
    attn = jax.vmap(partial(forward_head, scale=scale))(
        query_h, own_rows, paired_rows, cutoff_rows, live
    )
    attn_f = attn.astype(jnp.float32)
    grad_f = grad_h.astype(jnp.float32)
    gain = norm_gain.reshape(heads, 1, 1, width)
    square_part = jnp.sum(attn_f * attn_f, axis=(0, 3))
    mix_part = jnp.sum(gain * grad_f * attn_f, axis=(0, 3))
    square_sum, mix_sum = lax.psum((square_part, mix_part), "head")
    features = head_count * heads * width
    scale_row = lax.rsqrt(square_sum / features + 1e-06)[None, :, :, None]
    normed = (attn_f * scale_row * gain).astype(jnp.bfloat16)
    gain_part = jnp.sum(grad_f * attn_f * scale_row, axis=(1, 2))
    cotangent = (
        scale_row * gain * grad_f - attn_f * scale_row**3 * mix_sum[None, :, :, None] / features
    ).astype(jnp.bfloat16)
    query_grad, own_grad, pair_grad, cut_grad, top, total, delta = jax.vmap(
        partial(backward_head, scale=scale)
    )(query_h, own_rows, paired_rows, cutoff_rows, live, cotangent)
    cot_send = to_slots(cotangent, recv_slot, slot_count)
    cot_recv = lax.all_to_all(cot_send, "seq", split_axis=1, concat_axis=1, tiled=True)
    top_send = to_slots(top, recv_slot, slot_count)
    total_send = to_slots(total, recv_slot, slot_count)
    delta_send = to_slots(delta, recv_slot, slot_count)
    top_recv, total_recv, delta_recv = (
        lax.all_to_all(top_send, "seq", split_axis=1, concat_axis=1, tiled=True),
        lax.all_to_all(total_send, "seq", split_axis=1, concat_axis=1, tiled=True),
        lax.all_to_all(delta_send, "seq", split_axis=1, concat_axis=1, tiled=True),
    )
    pair_full = jax.vmap(partial(owner_pair, scale=scale))(
        query_owner,
        from_slots(cot_recv, send_slot),
        from_slots(top_recv, send_slot),
        from_slots(total_recv, send_slot),
        from_slots(delta_recv, send_slot),
        own_rows,
    )
    pair_term = lax.optimization_barrier(pair_full.astype(jnp.bfloat16)).astype(jnp.float32)
    cut_total, gain_total = lax.psum((cut_grad, gain_part), "seq")
    match = (
        (cut_dev == position)[:, :, None]
        & (cut_local[:, :, None] == jnp.arange(blocks)[None, None, :])
    ).astype(jnp.float32)
    cut_term = jnp.einsum("hcj,hcqd->hjqd", match, cut_total, precision=lax.Precision.HIGHEST)
    total_grad = (own_grad + pair_term + cut_term).astype(jnp.bfloat16)
    return (
        merge_heads(normed),
        merge_heads(query_grad),
        merge_heads(total_grad[..., :width]),
        merge_heads(total_grad[..., width:]),
        gain_total.reshape(heads * width),
    )


def solution(mesh):
    placed = (
        P("seq", "head"),
        P("seq", "head"),
        P("seq", "head"),
        P("seq", "head"),
        P("head", None),
        P("head"),
        P("head"),
    )
    return jax.shard_map(
        body,
        mesh=mesh,
        in_specs=placed,
        out_specs=(
            P("seq", "head"),
            P("seq", "head"),
            P("seq", "head"),
            P("seq", "head"),
            P("head"),
        ),
        check_vma=False,
    )
```

profile of v0, /device:TPU:0, one launch (start us, length us, event | category | flops | bytes accessed | tf_op | source)
XLA Modules:
  0.0 683.0 jit_solution(10543006544791201384)
XLA Ops:
  15.9 3.1 copy_select_fusion
  19.0 7.3 %all-to-all-start = ((bf16[2,8,256,256]{3,2,0,1:T(8,128)(2,1)}), bf16[2,8,256,256]{3,2,0,1:T(8,128)(2,1)}, u32[]{:S(2)}, u32[]{:S(2)}) async-start(bf16[2,8,256,256]{3,2,0,1:T(8,128)(2,1)} %copy_select_fusion), calls=%async_computation | async-start | bytes 4194304 | tf_op jit(solution)/shard_map/all_to_all | solution.py:286
  36.0 51.3 %all-to-all-done = bf16[2,8,256,256]{3,2,0,1:T(8,128)(2,1)} async-done(((bf16[2,8,256,256]{3,2,0,1:T(8,128)(2,1)}), bf16[2,8,256,256]{3,2,0,1:T(8,128)(2,1)}, u32[]{:S(2)}, u32[]{:S(2)}) %all-to-all-start) | async-done | bytes 2097184 | tf_op jit(solution)/shard_map/all_to_all | solution.py:286
  91.1 3.1 copy.276
  94.2 40.7 %all-reduce.5.cloned.1.call-done = bf16[2,4,256,256]{3,2,1,0:T(8,128)(2,1)} async-done(((bf16[2,4,256,256]{3,2,1,0:T(8,128)(2,1)}), bf16[2,4,256,256]{3,2,1,0:T(8,128)(2,1)}) %all-reduce.5.cloned.1.call-update) | async-done | bytes 1048592 | tf_op jit(solution)/shard_map/psum | solution.py:298
  136.1 76.6 %while.32 = (s32[]{:T(128)}, bf16[4,2,2,256,128]{4,3,2,0,1:T(8,128)(2,1)}, bf16[4,2,2,256,128]{4,3,2,1,0:T(8,128)(2,1)S(1)}, bf16[4,2,2,256,256]{4,3,2,1,0:T(8,1...) while((s32[]{:T(128)}, ...), condition=%wide.region_9.10_spmd.clone, body=%wide.region_6.9_spmd.clone.sunk | while | flops 818284032 | bytes 55597728 | solution.py:90
  142.7 5.4 copy.414
  148.3 3.7 fusion.235
  161.8 5.4 copy.414
  167.4 3.7 fusion.235
  181.0 5.4 copy.414
  186.6 3.7 fusion.235
  200.1 5.4 copy.414
  205.7 3.7 fusion.235
  217.2 6.9 %psum.36 = f32[8,256]{1,0:T(8,128)S(1)} all-reduce(f32[8,256]{1,0:T(8,128)S(1)} %reduce_sum.131), channel_id=1, replica_groups=mesh['seq'=8,'head'=4] {'head'}, use_global_device_ids=true, to_apply=%region_11.12 | all-reduce | flops 2048 | bytes 16384 | tf_op jit(solution)/shard_map/psum | solution.py:308
  227.0 6.3 psum.37
  233.3 3.2 fusion.113
  237.7 237.2 %while.33 = (s32[]{:T(128)}, f32[2,4,256,256]{2,3,1,0:T(8,128)}, bf16[4,2,2,256,128]{4,3,2,0,1:T(8,128)(2,1)}, f32[4,2,2,256,256]{3,4,2,1,0:T(8,128)}, f32[4,2,2...) while((s32[]{:T(128)}, f32[2,4,256,256]{2,3,1,0:T(8,128)}, ...), condition=%wide.region_18.19_spmd.clone, body=%wide.region_14.18_spmd.clone.sunk | while | flops 1934750720 | bytes 244144336 | solution.py:204
  243.4 5.4 copy.417
  258.1 5.4 copy.416
  263.5 5.6 multiply_reduce_fusion.3
  302.2 5.4 copy.417
  316.8 5.4 copy.416
  322.2 5.6 multiply_reduce_fusion.3
  352.4 3.5 maximum_add_fusion.2
  361.7 5.4 copy.417
  376.3 5.4 copy.416
  381.7 5.6 multiply_reduce_fusion.3
  411.9 3.5 maximum_add_fusion.2
  421.1 5.4 copy.417
  435.8 5.4 copy.416
  441.2 5.6 multiply_reduce_fusion.3
  471.4 3.5 maximum_add_fusion.2
  477.6 9.9 %all_to_all.30 = f32[2,8,256]{2,0,1:T(2,128)S(1)} all-to-all(f32[2,8,256]{2,0,1:T(2,128)S(1)} %get-tuple-element.372), channel_id=1, replica_groups=mesh['seq'=8,'head'=4] {'seq'}, dimensions={1} | all-to-all | bytes 32768 | tf_op jit(solution)/shard_map/all_to_all | solution.py:325
  487.5 3.3 all-to-all-start.3
  492.8 2.9 gather_fusion.9
  497.3 4.3 all-to-all-start.5
  501.6 3.0 copy_select_fusion.2
  504.6 3.6 all-to-all-done.5
  508.2 26.6 %all_to_all.31 = bf16[2,8,256,128]{3,2,0,1:T(8,128)(2,1)} all-to-all(bf16[2,8,256,128]{3,2,0,1:T(8,128)(2,1)} %get-tuple-element.373), channel_id=1, replica_groups=mesh['seq'=8,'head'=4] {'seq'}, dimensions={1} | all-to-all | bytes 2097152 | tf_op jit(solution)/shard_map/all_to_all | solution.py:287
  534.8 3.7 all-to-all-start.4
  540.5 4.6 copy.287
  549.6 28.1 %psum.39 = f32[256]{0:T(256)} all-reduce(f32[256]{0:T(256)S(1)} %bitcast.413), channel_id=1, replica_groups=mesh['seq'=8,'head'=4] {'seq'}, use_global_device_ids=true, to_apply=%region_23.24 | all-reduce | flops 256 | bytes 2048 | tf_op jit(solution)/shard_map/psum | solution.py:338
  587.4 4.8 fusion.121
  593.5 63.7 %all-reduce.7.cloned.1.call-done = f32[2,4,256,256]{3,1,2,0:T(4,128)} async-done(((f32[2,4,256,256]{3,1,2,0:T(4,128)}), f32[2,4,256,256]{3,1,2,0:T(4,128)}) %all-reduce.7.cloned.1.call-update) | async-done | bytes 2097168 | tf_op jit(solution)/shard_map/psum | solution.py:338
  657.2 5.3 fusion.130
  662.5 5.3 copy.306
  667.8 4.4 add_convert_fusion
  (454 shorter events, 259.1 us)
Async XLA Ops:
  15.9 10.5 %copy-start.31 = (s32[2,64]{1,0:T(2,128)S(1)}, s32[2,64]{1,0:T(2,128)}, u32[]{:S(2)}) copy-start(s32[2,64]{1,0:T(2,128)} %param.15) | copy-start | bytes 1540
  19.0 68.4 %all-to-all-start = ((bf16[2,8,256,256]{3,2,0,1:T(8,128)(2,1)}), bf16[2,8,256,256]{3,2,0,1:T(8,128)(2,1)}, u32[]{:S(2)}, u32[]{:S(2)}) async-start(bf16[2,8,256,256]{3,2,0,1:T(8,128)(2,1)} %copy_select_fusion), calls=%async_computation | async-start | bytes 4194304 | tf_op jit(solution)/shard_map/all_to_all | solution.py:286
  26.3 108.6 %all-reduce.5.cloned.1.call-start = ((), (), s32[]{:S(2)}) async-start(), calls=%async_computation.6 | async-start | bytes 2097152 | tf_op jit(solution)/shard_map/psum | solution.py:298
  89.1 47.0 %copy-start.42 = (s32[2]{0:T(128)S(1)}, s32[2]{0:T(128)}, u32[]{:S(2)}) copy-start(s32[2]{0:T(128)} %param.16) | copy-start | bytes 28
  212.7 11.5 %copy-start.19 = (f32[8,256,2,128]{3,2,1,0:T(2,128)S(1)}, f32[8,256,2,128]{3,2,1,0:T(2,128)}, u32[]{:S(2)}) copy-start(f32[8,256,2,128]{3,2,1,0:T(2,128)} %reshape.418) | copy-start | bytes 6291460
  212.7 11.5 %copy-start.41 = (f32[256]{0:T(256)S(1)}, f32[256]{0:T(256)}, u32[]{:S(2)}) copy-start(f32[256]{0:T(256)} %param.17) | copy-start | bytes 3076
  237.7 237.3 %copy-start.28 = (s32[16]{0:T(128)S(1)}, s32[16]{0:T(128)}, u32[]{:S(2)}) copy-start(s32[16]{0:T(128)} %reshape.321) | copy-start | bytes 196
  237.7 239.1 %copy-start.39 = (pred[2,8]{0,1:T(8,128)(4,1)S(1)}, pred[2,8]{0,1:T(8,128)(4,1)}, u32[]{:S(2)}) copy-start(pred[2,8]{0,1:T(8,128)(4,1)} %copy.288) | copy-start | bytes 52
  237.7 5.7 copy-start.7
  263.5 5.6 copy-start.1
  263.5 6.2 copy-start.2
  263.5 6.4 copy-start.6
  280.8 5.7 copy-start.8
  282.9 5.5 copy-start.5
  296.5 5.7 copy-start.7
  322.2 5.6 copy-start.1
  322.2 6.2 copy-start.2
  322.2 6.4 copy-start.6
  331.1 4.0 copy-start.3
  331.1 4.0 copy-start.4
  339.6 5.7 copy-start.8
  341.7 5.5 copy-start.5
  356.0 5.7 copy-start.7
  381.7 5.6 copy-start.1
  381.7 6.2 copy-start.2
  381.7 6.4 copy-start.6
  399.0 5.7 copy-start.8
  401.1 5.5 copy-start.5
  415.4 5.7 copy-start.7
  441.2 5.6 copy-start.1
  441.2 6.2 copy-start.2
  441.2 6.4 copy-start.6
  450.0 4.0 copy-start.3
  450.1 4.0 copy-start.4
  458.5 5.7 copy-start.8
  460.6 5.5 copy-start.5
  487.5 9.8 %all-to-all-start.3 = ((f32[2,8,256]{2,0,1:T(2,128)}), f32[2,8,256]{2,0,1:T(2,128)S(1)}, u32[]{:S(2)}, u32[]{:S(2)}) async-start(f32[2,8,256]{2,0,1:T(2,128)} %get-tuple-element.371), calls=%async_computation.3 | async-start | bytes 32768 | tf_op jit(solution)/shard_map/all_to_all | solution.py:326
  497.3 10.9 %all-to-all-start.5 = ((f32[2,8,256]{2,0,1:T(2,128)}), f32[2,8,256]{2,0,1:T(2,128)S(1)}, u32[]{:S(2)}, u32[]{:S(2)}) async-start(f32[2,8,256]{2,0,1:T(2,128)} %get-tuple-element.370), calls=%async_computation.5 | async-start | bytes 32768 | tf_op jit(solution)/shard_map/all_to_all | solution.py:327
  501.6 36.9 %copy-start.17 = (f32[2,4,256,256]{2,3,1,0:T(8,128)S(1)}, f32[2,4,256,256]{2,3,1,0:T(8,128)}, u32[]{:S(2)}) copy-start(f32[2,4,256,256]{2,3,1,0:T(8,128)} %get-tuple-element.120) | copy-start | bytes 6291460
  534.8 5.7 copy-start.34
  534.8 5.7 copy-start.36
  534.8 46.5 %all-to-all-start.4 = ((bf16[2,8,256,128]{3,2,0,1:T(8,128)(2,1)}), bf16[2,8,256,128]{3,2,0,1:T(8,128)(2,1)S(1)}, u32[]{:S(2)}, u32[]{:S(2)}) async-start(bf16[2,8,256,128]{3,2,0,1:T(8,128)(2,1)} %get-tuple-element.374), calls=%async_computation.4 | async-start | bytes 2097152 | tf_op jit(solution)/shard_map/all_to_all | solution.py:320
  538.5 118.7 %all-reduce.7.cloned.1.call-start = ((), (), s32[]{:S(2)}) async-start(), calls=%async_computation.7 | async-start | bytes 4194304 | tf_op jit(solution)/shard_map/psum | solution.py:338
  540.5 4.7 copy-start.25
  545.2 4.4 copy-start.40
  545.2 34.3 %copy-start.24 = (bf16[2,8,256,128]{3,2,0,1:T(8,128)(2,1)S(1)}, bf16[2,8,256,128]{3,2,0,1:T(8,128)(2,1)}, u32[]{:S(2)}) copy-start(bf16[2,8,256,128]{3,2,0,1:T(8,128)(2,1)} %all_to_all.31) | copy-start | bytes 3145732
  592.1 65.1 %copy-start.32 = (s32[2,4]{1,0:T(2,128)S(1)}, s32[2,4]{1,0:T(2,128)}, u32[]{:S(2)}) copy-start(s32[2,4]{1,0:T(2,128)} %get-tuple-element.351) | copy-start | bytes 100
  592.1 65.1 %copy-start.38 = (pred[2,4]{1,0:T(4,128)(4,1)S(1)}, pred[2,4]{1,0:T(4,128)(4,1)}, u32[]{:S(2)}) copy-start(pred[2,4]{1,0:T(4,128)(4,1)} %copy-done.37) | copy-start | bytes 28
  (55 other events, 128.4 us)
Sparse Core Ops, SparseCore 0:
  31.2 103.6 all-reduce.4
  542.9 114.2 all-reduce.6
where the time goes:
time: 686 us; the launch traced here: 683 us
  local copies, waits for them, and re-layouts  173 us (25%)
  waiting for transfers between devices  161 us (23%)
  matrix products  123 us (18%)
  other arithmetic  114 us (17%)
  blocking collectives  77.8 us (11%)
  starting transfers between devices  18.7 us (3%)
  between operations  14.6 us (2%)
    psum x1, waiting for transfers between devices, body(): cut_total, gain_total = lax.psum((cut_grad, gain_part), 'seq')  63.7 us
    all_to_all x1, waiting for transfers between devices, body(): lax.all_to_all(own_send, 'seq', split_axis=1, concat_axis=1, tiled=True)  51.3 us
    reshape x8, local copies, waits for them, and re-layouts, attend(): cut = cut.reshape(query.shape[0], query.shape[1], count * span)  43.2 us
    psum x1, waiting for transfers between devices, body(): lax.psum(cut_pick.astype(jnp.float32).astype(jnp.bfloat16), 'seq')  40.7 us
    psum x1, blocking collectives, body(): cut_total, gain_total = lax.psum((cut_grad, gain_part), 'seq')  28.1 us
    all_to_all x1, blocking collectives, body(): lax.all_to_all(query_send, 'seq', split_axis=1, concat_axis=1, tiled=True)  26.6 us
    reduce_sum x4, other arithmetic, backward_step(): delta = jnp.sum(prob * dprob, axis=-1)  22.4 us
    reshape x4, local copies, waits for them, and re-layouts, backward_step(): dprob = jnp.concatenate([jnp.einsum('gqd,gkd->gqk', cot_part, own_part[.....  21.7 us
  transfers between devices with their start and end apart: 6, of which 5 were waited for; matrix products, arithmetic and copies ran while one was open for 7% of the time, Pallas kernels for 0%

commit v1 on v0

--- a/solution.py
+++ b/solution.py
@@ -6,6 +6,18 @@
 
 BLOCK = 256
 KCUT = 4
+
+
+def rotated_exchange(value, axis, split, join):
+    ways, here = (lax.axis_size(axis), lax.axis_index(axis))
+    width = value.shape[split] // ways
+    turned = jnp.roll(value, -here * width, axis=split)
+    got = [lax.slice_in_dim(turned, 0, width, axis=split)]
+    for far in range(1, ways):
+        sent = lax.slice_in_dim(turned, far * width, (far + 1) * width, axis=split)
+        got.append(lax.ppermute(sent, axis, [(d, (d + far) % ways) for d in range(ways)]))
+    line = jnp.concatenate(got[::-1], axis=join)
+    return jnp.roll(line, (here + 1) * got[0].shape[join], axis=join)
 
 
 def split_heads(rows, heads):
@@ -283,7 +295,7 @@
     own_send = to_slots(own_rows, send_slot, slot_count)
     query_send = to_slots(query_h, recv_slot, slot_count)
     own_recv, query_recv = (
-        lax.all_to_all(own_send, "seq", split_axis=1, concat_axis=1, tiled=True),
+        rotated_exchange(own_send, "seq", 1, 1),
         lax.all_to_all(query_send, "seq", split_axis=1, concat_axis=1, tiled=True),
     )
     query_owner = from_slots(query_recv, send_slot)

time: 686 us -> 689 us (level)
    all_to_all x1 -> x0, waiting for transfers between devices: 51.3 us -> none  [body(): lax.all_to_all(own_send, 'seq', split_axis=1, concat_axis=1, tiled=True)]
    ppermute x0 -> x7, waiting for transfers between devices: none -> 37.8 us  [rotated_exchange(): lax.ppermute(sent, axis, [(d, (d + far) % ways) for d in range(ways)])]
    ppermute x0 -> x7, starting transfers between devices: none -> 12.5 us  [rotated_exchange(): lax.ppermute(sent, axis, [(d, (d + far) % ways) for d in range(ways)])]
    all_to_all x1 -> x0, starting transfers between devices: 7.28 us -> none  [body(): lax.all_to_all(own_send, 'seq', split_axis=1, concat_axis=1, tiled=True)]
    psum x1, waiting for transfers between devices: 40.7 us -> 47.7 us  [body(): lax.psum(cut_pick.astype(jnp.float32).astype(jnp.bfloat16), 'seq')]
    unnamed x61 -> x74, local copies, waits for them, and re-layouts: 17 us -> 22.6 us
  transfers between devices with their start and end apart: 6 -> 12, of which waited for: 5 -> 6; matrix products, arithmetic and copies ran while one was open for 7% -> 7% of each run, Pallas kernels for 0% -> 0%
where the time goes in v1:
time: 689 us; the launch traced here: 686 us
  local copies, waits for them, and re-layouts  177 us (26%)
  waiting for transfers between devices  158 us (23%)
  matrix products  124 us (18%)
  other arithmetic  111 us (16%)
  blocking collectives  76.9 us (11%)
  starting transfers between devices  22.7 us (3%)
  between operations  14.8 us (2%)
    psum x1, waiting for transfers between devices, body(): cut_total, gain_total = lax.psum((cut_grad, gain_part), 'seq')  64.2 us
    psum x1, waiting for transfers between devices, body(): lax.psum(cut_pick.astype(jnp.float32).astype(jnp.bfloat16), 'seq')  47.7 us
    reshape x8, local copies, waits for them, and re-layouts, attend(): cut = cut.reshape(query.shape[0], query.shape[1], count * span)  43.3 us
    ppermute x7, waiting for transfers between devices, rotated_exchange(): lax.ppermute(sent, axis, [(d, (d + far) % ways) for d in range(ways)])  37.8 us
    psum x1, blocking collectives, body(): cut_total, gain_total = lax.psum((cut_grad, gain_part), 'seq')  27.8 us
    all_to_all x1, blocking collectives, body(): lax.all_to_all(query_send, 'seq', split_axis=1, concat_axis=1, tiled=True)  26 us
    reduce_sum x4, other arithmetic, backward_step(): delta = jnp.sum(prob * dprob, axis=-1)  22.6 us
    unnamed x74, local copies, waits for them, and re-layouts  22.6 us
  transfers between devices with their start and end apart: 12, of which 6 were waited for; matrix products, arithmetic and copies ran while one was open for 7% of the time, Pallas kernels for 0%

profile of v1, /device:TPU:0, one launch (start us, length us, event | category | flops | bytes accessed | tf_op | source)
XLA Modules:
  0.0 686.1 jit_solution(5127588383337940336)
XLA Ops:
  21.4 6.0 collective-permute-start
  27.9 3.0 collective-permute-start.3
  45.4 4.1 collective-permute-done.2
  50.5 33.6 %collective-permute-done.3 = bf16[2,1,256,256]{3,2,1,0:T(8,128)(2,1)} collective-permute-done((bf16[2,1,256,256]{3,2,1,0:T(8,128)(2,1)}, bf16[2,1,256,256]{3,2,1,0:T(8,128)(2,1)}, u32[]{:S(2)}, u32[]{:S(2)}) %collective-permute-start.3) | collective-permute-done | bytes 262176 | tf_op jit(solution)/shard_map/ppermute | solution.py:18
  89.9 3.1 copy.271
  93.0 47.7 %all-reduce.5.cloned.1.call-done = bf16[2,4,256,256]{3,2,1,0:T(8,128)(2,1)} async-done(((bf16[2,4,256,256]{3,2,1,0:T(8,128)(2,1)}), bf16[2,4,256,256]{3,2,1,0:T(8,128)(2,1)}) %all-reduce.5.cloned.1.call-update) | async-done | bytes 1048592 | tf_op jit(solution)/shard_map/psum | solution.py:310
  141.9 76.7 %while.32 = (s32[]{:T(128)}, bf16[4,2,2,256,128]{4,3,2,0,1:T(8,128)(2,1)}, bf16[4,2,2,256,128]{4,3,2,1,0:T(8,128)(2,1)S(1)}, bf16[4,2,2,256,256]{4,3,2,1,0:T(8,1...) while((s32[]{:T(128)}, ...), condition=%wide.region_9.11_spmd.clone, body=%wide.region_6.10_spmd.clone.sunk | while | flops 818284032 | bytes 55597728 | solution.py:102
  148.5 5.4 copy.408
  154.1 3.7 fusion.238
  167.7 5.4 copy.408
  173.3 3.7 fusion.238
  186.9 5.4 copy.408
  192.5 3.7 fusion.238
  206.1 5.4 copy.408
  211.6 3.7 fusion.238
  223.1 7.1 %psum.36 = f32[8,256]{1,0:T(8,128)S(1)} all-reduce(f32[8,256]{1,0:T(8,128)S(1)} %reduce_sum.131), channel_id=1, replica_groups=mesh['seq'=8,'head'=4] {'head'}, use_global_device_ids=true, to_apply=%region_11.13 | all-reduce | flops 2048 | bytes 16384 | tf_op jit(solution)/shard_map/psum | solution.py:320
  233.1 6.1 psum.37
  239.2 3.2 fusion.115
  243.6 236.4 %while.33 = (s32[]{:T(128)}, f32[2,4,256,256]{2,3,1,0:T(8,128)}, bf16[4,2,2,256,128]{4,3,2,0,1:T(8,128)(2,1)}, f32[4,2,2,256,256]{3,4,2,1,0:T(8,128)}, f32[4,2,2...) while((s32[]{:T(128)}, f32[2,4,256,256]{2,3,1,0:T(8,128)}, ...), condition=%wide.region_18.20_spmd.clone, body=%wide.region_14.19_spmd.clone.sunk | while | flops 1934750720 | bytes 250435856 | solution.py:216
  249.4 5.4 copy.411
  264.2 5.4 copy.410
  269.6 5.7 multiply_reduce_fusion.3
  307.3 5.4 copy.411
  322.1 5.4 copy.410
  327.6 5.7 multiply_reduce_fusion.3
  357.8 3.2 maximum_add_fusion.2
  366.8 5.4 copy.411
  381.6 5.4 copy.410
  387.0 5.7 multiply_reduce_fusion.3
  417.3 3.2 maximum_add_fusion.2
  426.3 5.4 copy.411
  441.1 5.4 copy.410
  446.5 5.7 multiply_reduce_fusion.3
  476.8 3.2 maximum_add_fusion.2
  482.6 9.9 %all_to_all.25 = f32[2,8,256]{2,0,1:T(2,128)S(1)} all-to-all(f32[2,8,256]{2,0,1:T(2,128)S(1)} %get-tuple-element.380), channel_id=1, replica_groups=mesh['seq'=8,'head'=4] {'seq'}, dimensions={1} | all-to-all | bytes 32768 | tf_op jit(solution)/shard_map/all_to_all | solution.py:337
  492.5 3.3 all-to-all-start.2
  498.6 3.8 all-to-all-done.2
  502.4 3.3 all-to-all-start.4
  507.3 4.9 all-to-all-done.4
  512.2 26.0 %all_to_all.26 = bf16[2,8,256,128]{3,2,0,1:T(8,128)(2,1)} all-to-all(bf16[2,8,256,128]{3,2,0,1:T(8,128)(2,1)} %get-tuple-element.381), channel_id=1, replica_groups=mesh['seq'=8,'head'=4] {'seq'}, dimensions={1} | all-to-all | bytes 2097152 | tf_op jit(solution)/shard_map/all_to_all | solution.py:299
  538.2 3.6 all-to-all-start.3
  543.9 4.7 copy.282
  553.0 27.8 %psum.39 = f32[256]{0:T(256)} all-reduce(f32[256]{0:T(256)S(1)} %bitcast.413), channel_id=1, replica_groups=mesh['seq'=8,'head'=4] {'seq'}, use_global_device_ids=true, to_apply=%region_23.25 | all-reduce | flops 256 | bytes 2048 | tf_op jit(solution)/shard_map/psum | solution.py:350
  590.0 4.8 fusion.123
  596.2 64.2 %all-reduce.7.cloned.1.call-done = f32[2,4,256,256]{3,1,2,0:T(4,128)} async-done(((f32[2,4,256,256]{3,1,2,0:T(4,128)}), f32[2,4,256,256]{3,1,2,0:T(4,128)}) %all-reduce.7.cloned.1.call-update) | async-done | bytes 2097168 | tf_op jit(solution)/shard_map/psum | solution.py:350
  660.3 5.3 fusion.132
  665.6 5.3 copy.301
  670.9 4.4 add_convert_fusion
  (496 shorter events, 272.8 us)
Async XLA Ops:
  7.2 133.6 %all-reduce.5.cloned.1.call-start = ((), (), s32[]{:S(2)}) async-start(), calls=%async_computation.5 | async-start | bytes 2097152 | tf_op jit(solution)/shard_map/psum | solution.py:310
  18.2 12.7 %copy-start.36 = (s32[2,64]{1,0:T(2,128)S(1)}, s32[2,64]{1,0:T(2,128)}, u32[]{:S(2)}) copy-start(s32[2,64]{1,0:T(2,128)} %param.17) | copy-start | bytes 1540
  21.4 19.0 %collective-permute-start = (bf16[2,1,256,256]{3,2,1,0:T(8,128)(2,1)}, bf16[2,1,256,256]{3,2,1,0:T(8,128)(2,1)}, u32[]{:S(2)}, u32[]{:S(2)}) collective-permute-start(bf16[2,1,256,256]{3,2,1,0:T(8,128)(2,1)} %get-tuple-element.373), channel_id=1, source_target_pairs={{0,28},{4,0},{8,4},{12,8},{16,12},{20,16},{24,20},{28,24},{1,29},{... | collective-permute-start | bytes 786440 | tf_op jit(solution)/shard_map/ppermute | solution.py:18
  27.4 15.8 %collective-permute-start.1 = (bf16[2,1,256,256]{3,2,1,0:T(8,128)(2,1)}, bf16[2,1,256,256]{3,2,1,0:T(8,128)(2,1)}, u32[]{:S(2)}, u32[]{:S(2)}) collective-permute-start(bf16[2,1,256,256]{3,2,1,0:T(8,128)(2,1)} %get-tuple-element.372), channel_id=1, source_target_pairs={{0,24},{4,28},{8,0},{12,4},{16,8},{20,12},{24,16},{28,20},{1,25},{... | collective-permute-start | bytes 786440 | tf_op jit(solution)/shard_map/ppermute | solution.py:18
  27.9 21.6 %collective-permute-start.2 = (bf16[2,1,256,256]{3,2,1,0:T(8,128)(2,1)}, bf16[2,1,256,256]{3,2,1,0:T(8,128)(2,1)}, u32[]{:S(2)}, u32[]{:S(2)}) collective-permute-start(bf16[2,1,256,256]{3,2,1,0:T(8,128)(2,1)} %get-tuple-element.371), channel_id=1, source_target_pairs={{0,20},{4,24},{8,28},{12,0},{16,4},{20,8},{24,12},{28,16},{1,21},{... | collective-permute-start | bytes 786440 | tf_op jit(solution)/shard_map/ppermute | solution.py:18
  27.9 56.2 %collective-permute-start.3 = (bf16[2,1,256,256]{3,2,1,0:T(8,128)(2,1)}, bf16[2,1,256,256]{3,2,1,0:T(8,128)(2,1)}, u32[]{:S(2)}, u32[]{:S(2)}) collective-permute-start(bf16[2,1,256,256]{3,2,1,0:T(8,128)(2,1)} %get-tuple-element.370), channel_id=1, source_target_pairs={{0,16},{4,20},{8,24},{12,28},{16,0},{20,4},{24,8},{28,12},{1,17},{... | collective-permute-start | bytes 786440 | tf_op jit(solution)/shard_map/ppermute | solution.py:18
  30.9 54.2 %collective-permute-start.4 = (bf16[2,1,256,256]{3,2,1,0:T(8,128)(2,1)}, bf16[2,1,256,256]{3,2,1,0:T(8,128)(2,1)}, u32[]{:S(2)}, u32[]{:S(2)}) collective-permute-start(bf16[2,1,256,256]{3,2,1,0:T(8,128)(2,1)} %get-tuple-element.369), channel_id=1, source_target_pairs={{0,12},{4,16},{8,20},{12,24},{16,28},{20,0},{24,4},{28,8},{1,13},{... | collective-permute-start | bytes 786440 | tf_op jit(solution)/shard_map/ppermute | solution.py:18
  40.4 45.6 %collective-permute-start.5 = (bf16[2,1,256,256]{3,2,1,0:T(8,128)(2,1)S(1)}, bf16[2,1,256,256]{3,2,1,0:T(8,128)(2,1)S(1)}, u32[]{:S(2)}, u32[]{:S(2)}) collective-permute-start(bf16[2,1,256,256]{3,2,1,0:T(8,128)(2,1)S(1)} %copy-done.35), channel_id=1, source_target_pairs={{0,8},{4,12},{8,16},{12,20},{16,24},{20,28},{24,0},{28,4},{1,9},{5... | collective-permute-start | bytes 786440 | tf_op jit(solution)/shard_map/ppermute | solution.py:18
  43.2 42.9 %collective-permute-start.6 = (bf16[2,1,256,256]{3,2,1,0:T(8,128)(2,1)S(1)}, bf16[2,1,256,256]{3,2,1,0:T(8,128)(2,1)S(1)}, u32[]{:S(2)}, u32[]{:S(2)}) collective-permute-start(bf16[2,1,256,256]{3,2,1,0:T(8,128)(2,1)S(1)} %get-tuple-element.367), channel_id=1, source_target_pairs={{0,4},{4,8},{8,12},{12,16},{16,20},{20,24},{24,28},{28,0},{1,5},{5... | collective-permute-start | bytes 786440 | tf_op jit(solution)/shard_map/ppermute | solution.py:18
  89.9 52.0 %copy-start.47 = (s32[2]{0:T(128)S(1)}, s32[2]{0:T(128)}, u32[]{:S(2)}) copy-start(s32[2]{0:T(128)} %param.18) | copy-start | bytes 28
  218.6 11.7 %copy-start.22 = (f32[8,256,2,128]{3,2,1,0:T(2,128)S(1)}, f32[8,256,2,128]{3,2,1,0:T(2,128)}, u32[]{:S(2)}) copy-start(f32[8,256,2,128]{3,2,1,0:T(2,128)} %reshape.418) | copy-start | bytes 6291460
  218.6 11.7 %copy-start.46 = (f32[256]{0:T(256)S(1)}, f32[256]{0:T(256)}, u32[]{:S(2)}) copy-start(f32[256]{0:T(256)} %param.19) | copy-start | bytes 3076
  243.6 236.5 %copy-start.32 = (s32[16]{0:T(128)S(1)}, s32[16]{0:T(128)}, u32[]{:S(2)}) copy-start(s32[16]{0:T(128)} %reshape.321) | copy-start | bytes 196
  243.6 238.3 %copy-start.44 = (pred[2,8]{0,1:T(8,128)(4,1)S(1)}, pred[2,8]{0,1:T(8,128)(4,1)}, u32[]{:S(2)}) copy-start(pred[2,8]{0,1:T(8,128)(4,1)} %copy.283) | copy-start | bytes 52
  243.6 5.7 copy-start.7
  269.6 5.7 copy-start.1
  269.6 6.2 copy-start.2
  269.6 6.4 copy-start.6
  287.0 5.7 copy-start.8
  289.1 5.4 copy-start.5
  301.6 5.7 copy-start.7
  327.5 5.7 copy-start.1
  327.6 6.2 copy-start.2
  327.6 6.4 copy-start.6
  344.9 5.7 copy-start.8
  347.0 5.4 copy-start.5
  361.0 5.7 copy-start.7
  387.0 5.7 copy-start.1
  387.0 6.2 copy-start.2
  387.0 6.4 copy-start.6
  404.4 5.7 copy-start.8
  406.5 5.4 copy-start.5
  420.5 5.7 copy-start.7
  446.5 5.7 copy-start.1
  446.5 6.2 copy-start.2
  446.5 6.4 copy-start.6
  463.9 5.7 copy-start.8
  466.0 5.4 copy-start.5
  480.0 17.8 %copy-start.21 = (bf16[4,2,2,256,128]{4,3,2,0,1:T(8,128)(2,1)S(1)}, bf16[4,2,2,256,128]{4,3,2,0,1:T(8,128)(2,1)}, u32[]{:S(2)}) copy-start(bf16[4,2,2,256,128]{4,3,2,0,1:T(8,128)(2,1)} %get-tuple-element.606) | copy-start | bytes 3145732
  492.5 9.8 %all-to-all-start.2 = ((f32[2,8,256]{2,0,1:T(2,128)}), f32[2,8,256]{2,0,1:T(2,128)S(1)}, u32[]{:S(2)}, u32[]{:S(2)}) async-start(f32[2,8,256]{2,0,1:T(2,128)} %get-tuple-element.379), calls=%async_computation.2 | async-start | bytes 32768 | tf_op jit(solution)/shard_map/all_to_all | solution.py:338
  502.4 9.8 %all-to-all-start.4 = ((f32[2,8,256]{2,0,1:T(2,128)}), f32[2,8,256]{2,0,1:T(2,128)S(1)}, u32[]{:S(2)}, u32[]{:S(2)}) async-start(f32[2,8,256]{2,0,1:T(2,128)} %get-tuple-element.378), calls=%async_computation.4 | async-start | bytes 32768 | tf_op jit(solution)/shard_map/all_to_all | solution.py:339
  507.3 34.5 %copy-start.19 = (f32[2,4,256,256]{2,3,1,0:T(8,128)S(1)}, f32[2,4,256,256]{2,3,1,0:T(8,128)}, u32[]{:S(2)}) copy-start(f32[2,4,256,256]{2,3,1,0:T(8,128)} %get-tuple-element.121) | copy-start | bytes 6291460
  538.2 46.1 %all-to-all-start.3 = ((bf16[2,8,256,128]{3,2,0,1:T(8,128)(2,1)}), bf16[2,8,256,128]{3,2,0,1:T(8,128)(2,1)S(1)}, u32[]{:S(2)}, u32[]{:S(2)}) async-start(bf16[2,8,256,128]{3,2,0,1:T(8,128)(2,1)} %get-tuple-element.382), calls=%async_computation.3 | async-start | bytes 2097152 | tf_op jit(solution)/shard_map/all_to_all | solution.py:332
  541.8 118.6 %all-reduce.7.cloned.1.call-start = ((), (), s32[]{:S(2)}) async-start(), calls=%async_computation.6 | async-start | bytes 4194304 | tf_op jit(solution)/shard_map/psum | solution.py:350
  543.9 4.7 copy-start.29
  549.6 32.9 %copy-start.28 = (bf16[2,8,256,128]{3,2,0,1:T(8,128)(2,1)S(1)}, bf16[2,8,256,128]{3,2,0,1:T(8,128)(2,1)}, u32[]{:S(2)}) copy-start(bf16[2,8,256,128]{3,2,0,1:T(8,128)(2,1)} %all_to_all.26) | copy-start | bytes 3145732
  594.8 65.6 %copy-start.37 = (s32[2,4]{1,0:T(2,128)S(1)}, s32[2,4]{1,0:T(2,128)}, u32[]{:S(2)}) copy-start(s32[2,4]{1,0:T(2,128)} %get-tuple-element.352) | copy-start | bytes 100
  594.8 65.6 %copy-start.43 = (pred[2,4]{1,0:T(4,128)(4,1)S(1)}, pred[2,4]{1,0:T(4,128)(4,1)}, u32[]{:S(2)}) copy-start(pred[2,4]{1,0:T(4,128)(4,1)} %copy-done.42) | copy-start | bytes 28
  (72 other events, 170.4 us)
Sparse Core Ops, SparseCore 0:
  33.4 107.2 all-reduce.4
  546.2 114.0 all-reduce.6
